TPU v7x, 512 devices: a whole 4x4x16 slice. The times are simulated.
512 devices in a mesh: seq: 512 (over y, z, x, core).
Axes of the slice: x: 4, y: 4, z: 16, core: 2. Of those that a mesh axis runs over, the one named last changes fastest.
Arguments:
- queries: bfloat16 [98304, 1024], P('seq'), may hold values from -200 to 200
- keyval: bfloat16 [2, 98304, 128], P(None, 'seq'), may hold values from -7 to 7
Outputs:
- attended: bfloat16 [98304, 1024], P('seq')
All inputs are finite; a program needn't handle non-finite values.
Results may differ from a plain program's by a relative error of at most 0.0029.
Values may be sent and summed in bfloat16 or wider, within the bound.
A program may use at most 64 MiB of HBM per device.

v0:
```python
import jax
import jax.numpy as jnp
from jax import lax
from jax.sharding import PartitionSpec as P

QH = 8
KVH = 1
HD = 128


def partner(block, axis, stride):
    count = lax.axis_size(axis)
    route = []
    for low in range(count):
        high = low | 1 << stride
        if high != low and high < count:
            route += [(low, high), (high, low)]
    return lax.ppermute(block, axis, route)


def spread(value, axis, source):
    kept = jnp.where(lax.axis_index(axis) == source, value, 0).astype(value.dtype)
    return lax.psum(kept, axis)


def attend(queries, keyval):
    tok = queries.shape[0]
    total = keyval.shape[1]
    group = QH // KVH
    scale = 1.0 / HD**0.5
    qs = jnp.moveaxis(queries.reshape(tok, KVH, group * HD), 1, 0)
    ks = jnp.moveaxis(keyval[0].reshape(total, KVH, HD), 1, 0)
    vs = jnp.moveaxis(keyval[1].reshape(total, KVH, HD), 1, 0)

    def per_head(items):
        q_group, k_head, v_head = items
        q_group = q_group.reshape(tok, group, HD)
        scores = (
            jnp.einsum("tqd,sd->qts", q_group, k_head, preferred_element_type=jnp.float32) * scale
        )
        top = jnp.max(scores, axis=2, keepdims=True)
        probs = jnp.exp(scores - top)
        totals = jnp.sum(probs, axis=2)
        weights = probs.astype(jnp.bfloat16)
        summed = jnp.einsum("qts,sd->tqd", weights, v_head, preferred_element_type=jnp.float32)
        return summed / jnp.moveaxis(totals, 0, 1)[:, :, None]

    outs = lax.map(per_head, (qs, ks, vs))
    return jnp.moveaxis(outs, 0, 1).reshape(tok, QH * HD).astype(jnp.bfloat16)


def on_device(queries, keyval):
    levels = lax.axis_size("seq").bit_length() - 1
    bit_list = list(range(levels))
    received = {}
    for bit in bit_list:
        received[bit] = partner(keyval, "seq", bit)
    first = spread(keyval, "seq", 0)
    pieces = [keyval] + [received[bit] for bit in range(levels)] + [first]
    gathered = jnp.concatenate(pieces, axis=1)
    return attend(queries, gathered)


def solution(mesh):
    return jax.shard_map(
        on_device,
        mesh=mesh,
        in_specs=(P("seq", None), P(None, "seq", None)),
        out_specs=P("seq", None),
        check_vma=False,
    )
```

profile of v0, /device:TPU:1, one launch (start us, length us, event | category | flops | bytes accessed | tf_op | source)
XLA Modules:
  0.0 501.1 jit_solution(14704706188251303383)
XLA Ops:
  6.5 4.1 collective-permute-start.7
  10.7 15.4 %collective-permute-start.6 = (bf16[2,192,128]{2,1,0:T(8,128)(2,1)}, bf16[2,192,128]{2,1,0:T(8,128)(2,1)S(1)}, u32[]{:S(2)}, u32[]{:S(2)}) collective-permute-start(bf16[2,192,128]{2,1,0:T(8,128)(2,1)} %param.3), channel_id=1, source_target_pairs={{0,64},{64,0},{1,65},{65,1},{2,66},{66,2},{3,67},{67,3},{4,68},{68... | collective-permute-start | bytes 294920 | tf_op jit(solution)/shard_map/ppermute | solution.py:18
  26.1 4.0 collective-permute-start.5
  30.2 3.1 collective-permute-start.4
  33.3 3.7 collective-permute-start
  37.0 1.6 broadcast_select_fusion
  38.6 3.1 collective-permute-start.1
  41.8 0.7 constant_dynamic-update-slice_fusion.9
  42.4 2.7 collective-permute-done.1
  45.1 4.6 collective-permute-start.2
  50.4 1.8 collective-permute-done.2
  52.1 2.6 collective-permute-start.3
  55.4 2.7 collective-permute-done.3
  58.1 4.1 collective-permute-start.8
  62.2 0.7 constant_dynamic-update-slice_fusion.6
  63.6 0.6 constant_dynamic-update-slice_fusion.4
  64.2 0.7 constant_dynamic-update-slice_fusion.3
  64.9 0.7 constant_dynamic-update-slice_fusion.2
  66.2 416.8 %all-reduce.2.cloned.1.call-done = bf16[2,192,128]{2,1,0:T(8,128)(2,1)} async-done(((bf16[2,192,128]{2,1,0:T(8,128)(2,1)}), bf16[2,192,128]{2,1,0:T(8,128)(2,1)}) %all-reduce.2.cloned.1.call-update) | async-done | bytes 98320 | tf_op jit(solution)/shard_map/psum | solution.py:23
  483.0 1.6 constant_dynamic-update-slice_fusion
  484.5 3.1 bitcast_reduce_fusion
  487.6 2.3 fusion.1
  490.0 3.4 fusion.14
  493.4 0.9 copy.15
  (14 shorter events, 2.6 us)
Async XLA Ops:
  6.5 478.0 %copy-start = (bf16[192,1024]{1,0:T(8,128)(2,1)S(1)}, bf16[192,1024]{1,0:T(8,128)(2,1)}, u32[]{:S(2)}) copy-start(bf16[192,1024]{1,0:T(8,128)(2,1)} %param.2) | copy-start | bytes 1179652
  6.5 476.4 %all-reduce.2.cloned.1.call-start = ((), (), s32[]{:S(2)}) async-start(), calls=%async_computation | async-start | bytes 196608 | tf_op jit(solution)/shard_map/psum | solution.py:23
  6.5 58.3 %collective-permute-start.7 = (bf16[2,192,128]{2,1,0:T(8,128)(2,1)}, bf16[2,192,128]{2,1,0:T(8,128)(2,1)S(1)}, u32[]{:S(2)}, u32[]{:S(2)}) collective-permute-start(bf16[2,192,128]{2,1,0:T(8,128)(2,1)} %param.3), channel_id=1, source_target_pairs={{0,128},{128,0},{1,129},{129,1},{2,130},{130,2},{3,131},{131,3},{4... | collective-permute-start | bytes 294920 | tf_op jit(solution)/shard_map/ppermute | solution.py:18
  10.7 53.5 %collective-permute-start.6 = (bf16[2,192,128]{2,1,0:T(8,128)(2,1)}, bf16[2,192,128]{2,1,0:T(8,128)(2,1)S(1)}, u32[]{:S(2)}, u32[]{:S(2)}) collective-permute-start(bf16[2,192,128]{2,1,0:T(8,128)(2,1)} %param.3), channel_id=1, source_target_pairs={{0,64},{64,0},{1,65},{65,1},{2,66},{66,2},{3,67},{67,3},{4,68},{68... | collective-permute-start | bytes 294920 | tf_op jit(solution)/shard_map/ppermute | solution.py:18
  26.1 37.4 %collective-permute-start.5 = (bf16[2,192,128]{2,1,0:T(8,128)(2,1)}, bf16[2,192,128]{2,1,0:T(8,128)(2,1)S(1)}, u32[]{:S(2)}, u32[]{:S(2)}) collective-permute-start(bf16[2,192,128]{2,1,0:T(8,128)(2,1)} %param.3), channel_id=1, source_target_pairs={{0,32},{32,0},{1,33},{33,1},{2,34},{34,2},{3,35},{35,3},{4,36},{36... | collective-permute-start | bytes 294920 | tf_op jit(solution)/shard_map/ppermute | solution.py:18
  30.2 32.7 %collective-permute-start.4 = (bf16[2,192,128]{2,1,0:T(8,128)(2,1)}, bf16[2,192,128]{2,1,0:T(8,128)(2,1)S(1)}, u32[]{:S(2)}, u32[]{:S(2)}) collective-permute-start(bf16[2,192,128]{2,1,0:T(8,128)(2,1)} %param.3), channel_id=1, source_target_pairs={{0,16},{16,0},{1,17},{17,1},{2,18},{18,2},{3,19},{19,3},{4,20},{20... | collective-permute-start | bytes 294920 | tf_op jit(solution)/shard_map/ppermute | solution.py:18
  33.3 5.3 %collective-permute-start = (bf16[2,192,128]{2,1,0:T(8,128)(2,1)}, bf16[2,192,128]{2,1,0:T(8,128)(2,1)S(1)}, u32[]{:S(2)}, u32[]{:S(2)}) collective-permute-start(bf16[2,192,128]{2,1,0:T(8,128)(2,1)} %param.3), channel_id=1, source_target_pairs={{0,1},{1,0},{2,3},{3,2},{4,5},{5,4},{6,7},{7,6},{8,9},{9,8},{10,11... | collective-permute-start | bytes 294920 | tf_op jit(solution)/shard_map/ppermute | solution.py:18
  38.6 6.4 %collective-permute-start.1 = (bf16[2,192,128]{2,1,0:T(8,128)(2,1)}, bf16[2,192,128]{2,1,0:T(8,128)(2,1)S(1)}, u32[]{:S(2)}, u32[]{:S(2)}) collective-permute-start(bf16[2,192,128]{2,1,0:T(8,128)(2,1)} %param.3), channel_id=1, source_target_pairs={{0,2},{2,0},{1,3},{3,1},{4,6},{6,4},{5,7},{7,5},{8,10},{10,8},{9,1... | collective-permute-start | bytes 294920 | tf_op jit(solution)/shard_map/ppermute | solution.py:18
  45.1 7.1 %collective-permute-start.2 = (bf16[2,192,128]{2,1,0:T(8,128)(2,1)}, bf16[2,192,128]{2,1,0:T(8,128)(2,1)S(1)}, u32[]{:S(2)}, u32[]{:S(2)}) collective-permute-start(bf16[2,192,128]{2,1,0:T(8,128)(2,1)} %param.3), channel_id=1, source_target_pairs={{0,4},{4,0},{1,5},{5,1},{2,6},{6,2},{3,7},{7,3},{8,12},{12,8},{9,1... | collective-permute-start | bytes 294920 | tf_op jit(solution)/shard_map/ppermute | solution.py:18
  52.1 6.0 %collective-permute-start.3 = (bf16[2,192,128]{2,1,0:T(8,128)(2,1)}, bf16[2,192,128]{2,1,0:T(8,128)(2,1)S(1)}, u32[]{:S(2)}, u32[]{:S(2)}) collective-permute-start(bf16[2,192,128]{2,1,0:T(8,128)(2,1)} %param.3), channel_id=1, source_target_pairs={{0,8},{8,0},{1,9},{9,1},{2,10},{10,2},{3,11},{11,3},{4,12},{12,4},... | collective-permute-start | bytes 294920 | tf_op jit(solution)/shard_map/ppermute | solution.py:18
  58.1 7.4 %collective-permute-start.8 = (bf16[2,192,128]{2,1,0:T(8,128)(2,1)}, bf16[2,192,128]{2,1,0:T(8,128)(2,1)S(1)}, u32[]{:S(2)}, u32[]{:S(2)}) collective-permute-start(bf16[2,192,128]{2,1,0:T(8,128)(2,1)} %param.3), channel_id=1, source_target_pairs={{0,256},{256,0},{1,257},{257,1},{2,258},{258,2},{3,259},{259,3},{4... | collective-permute-start | bytes 294920 | tf_op jit(solution)/shard_map/ppermute | solution.py:18
Sparse Core Ops, SparseCore 0:
  38.7 444.1 all-reduce.1
where the time goes:
time: 502 us; the launch traced here: 501 us
  waiting for transfers between devices  424 us (84%)
  starting transfers between devices  44.9 us (9%)
  between operations  13.5 us (3%)
  local copies, waits for them, and re-layouts  8.27 us (2%)
  matrix products  6.54 us (1%)
    psum x1, waiting for transfers between devices, spread(): return lax.psum(kept, axis)  417 us
    ppermute x9, starting transfers between devices, partner(): return lax.ppermute(block, axis, route)  44.9 us
  transfers between devices with their start and end apart: 10, of which 4 were waited for; matrix products, arithmetic and copies ran while one was open for 1% of the time, Pallas kernels for 0%

commit v1 on v0

v1 whole, which is shorter than its diff:
```python
import functools
import math

import jax
import jax.numpy as jnp
from jax import lax
from jax.experimental import pallas as pl
from jax.experimental.pallas import tpu as pltpu
from jax.sharding import PartitionSpec as P

HEADS = 8
HD = 128
TOK = 192
PAIR = 2 * TOK
PAIRS = HEADS // 2
SLOTS = 11
FIRST = 10
LOG2E = math.log2(math.e)
SCALE = LOG2E / math.sqrt(HD)
DIRECT = (5, 4, 3, 2, 8, 1, 7, 0)
FAR, RELAY = 6, 5
VISIT = (0, 1, 7, 3, 2, 8, 4)


def index_of(y, z, x, c):
    return ((y * 16 + z) * 4 + x) * 2 + c


def kernel(q_hbm, kv_hbm, out_ref, q_ref, kv_ref, qt_ref, m_ref, l_ref, acc_ref,
           q_sem, send_sem, recv_sem, tree_sem):
    me = lax.axis_index("seq")
    c = me % 2
    x = (me // 2) % 4
    z = (me // 8) % 16
    y = me // 128

    def partner(bit):
        stride = 1 << bit
        return me + stride * (1 - 2 * ((me // stride) % 2))

    def shifted(dz):
        return index_of(y, (z + dz) % 16, x, c)

    far_z = (z % 4) + 4 * (3 - z // 4)
    far = index_of(y, far_z, x, c)

    base = c == 0
    plane = jnp.logical_and(base, z == 0)
    row = jnp.logical_and(plane, y == 0)
    root = jnp.logical_and(row, x == 0)
    children = []
    for dx in (2, 1, 3):
        children.append((root, index_of(0, 0, dx, 0)))
    for dy in (2, 1, 3):
        children.append((row, index_of(dy, 0, x, 0)))
    for dz in (4, 12, 2, 14, 1, 15):
        children.append((plane, index_of(y, dz, x, 0)))
    for parent, dz in ((4, 8), (4, 7), (4, 6), (4, 5), (12, 9), (12, 10), (12, 11), (2, 3), (14, 13)):
        children.append((jnp.logical_and(base, z == parent), index_of(y, dz, x, 0)))
    children.append((base, index_of(y, z, x, 1)))

    up = jnp.where(z <= 8, 4, 12)
    up = jnp.where(z == 3, 2, jnp.where(z == 13, 14, up))
    up = jnp.where((z <= 2) | (z == 4) | (z == 12) | (z >= 14), 0, up)
    parent = jnp.where(
        c == 1, index_of(y, z, x, 0),
        jnp.where(z != 0, index_of(y, up, x, 0),
                  jnp.where(y != 0, index_of(0, 0, x, 0), 0)))

    is_root = me == 0
    q_copy = pltpu.make_async_copy(q_hbm, q_ref, q_sem.at[0])
    own_copy = pltpu.make_async_copy(kv_hbm, kv_ref.at[0], q_sem.at[1])
    own_copy.start()
    q_copy.start()

    barrier = pltpu.get_barrier_semaphore()
    for bit in DIRECT:
        pl.semaphore_signal(barrier, inc=1, device_id=(partner(bit),), device_id_type=pl.DeviceIdType.MESH)
    pl.semaphore_signal(barrier, inc=1, device_id=(far,), device_id_type=pl.DeviceIdType.MESH)

    @pl.when(jnp.logical_not(is_root))
    def _():
        pl.semaphore_signal(barrier, inc=1, device_id=(parent,), device_id_type=pl.DeviceIdType.MESH)

    def remote(src, dst, send, recv, target):
        return pltpu.make_async_remote_copy(
            src_ref=kv_ref.at[src], dst_ref=kv_ref.at[dst], send_sem=send, recv_sem=recv,
            device_id=(target,), device_id_type=pl.DeviceIdType.MESH)

    def direct(bit):
        return remote(0, 1 + bit, send_sem.at[bit], recv_sem.at[1 + bit], partner(bit))

    def relay():
        return remote(1 + RELAY, 1 + FAR, send_sem.at[FAR], recv_sem.at[1 + FAR], far)

    def down(i, src):
        return remote(src, FIRST, tree_sem.at[i], recv_sem.at[FIRST], children[i][1])

    def arrived(slot):
        pltpu.make_async_copy(kv_ref.at[slot], kv_ref.at[slot], recv_sem.at[slot]).wait()

    def attend(slot):
        vt = kv_ref[slot, 1].T

        @pl.loop(0, PAIRS)
        def _(pair):
            s = jnp.dot(kv_ref[slot, 0], qt_ref[pair], preferred_element_type=jnp.float32)
            top = jnp.max(s, axis=0, keepdims=True)
            if slot == 0:
                new = top
            else:
                old = m_ref[pair]
                new = jnp.maximum(old, top)
            p = jnp.exp2((s - new) * SCALE)
            total = jnp.sum(p, axis=0, keepdims=True)
            part = jnp.dot(vt, p.astype(jnp.bfloat16), preferred_element_type=jnp.float32)
            m_ref[pair] = new
            if slot == 0:
                l_ref[pair] = total
                acc_ref[pair] = part
            else:
                fade = jnp.exp2((old - new) * SCALE)
                l_ref[pair] = l_ref[pair] * fade + total
                acc_ref[pair] = acc_ref[pair] * fade + part

    q_copy.wait()
    for pair in range(PAIRS):
        both = jnp.concatenate(
            [q_ref[:, (2 * pair + h) * HD:(2 * pair + h + 1) * HD] for h in range(2)], axis=0)
        qt_ref[pair] = both.T
    own_copy.wait()
    attend(0)

    expected = 9
    for condition, _ in children:
        expected = expected + condition.astype(jnp.int32)
    pl.semaphore_wait(barrier, expected)

    def pass_down(src):
        for i, (condition, _) in enumerate(children):
            @pl.when(condition)
            def _(i=i):
                down(i, src).start()

    @pl.when(is_root)
    def _():
        pass_down(0)

    for bit in DIRECT:
        direct(bit).start()

    def take_first():
        arrived(FIRST)
        pass_down(FIRST)

    level = jnp.where(base, jnp.where(z == 0, 0, jnp.where((z == 4) | (z == 12) | (z == 2) | (z == 14), 1, 2)), 2)

    @pl.when(jnp.logical_and(level == 0, jnp.logical_not(is_root)))
    def _():
        take_first()

    for bit in VISIT:
        arrived(1 + bit)
        attend(1 + bit)

    arrived(1 + RELAY)
    relay().start()

    @pl.when(level == 1)
    def _():
        take_first()

    attend(1 + RELAY)
    attend_late = 2

    arrived(1 + FAR)
    attend(1 + FAR)

    @pl.when(level == attend_late)
    def _():
        take_first()

    @pl.when(is_root)
    def _():
        local = pltpu.make_async_copy(kv_ref.at[0], kv_ref.at[FIRST], q_sem.at[0])
        local.start()
        local.wait()

    attend(FIRST)

    for pair in range(PAIRS):
        both = (acc_ref[pair] / l_ref[pair]).T
        for h in range(2):
            out_ref[:, (2 * pair + h) * HD:(2 * pair + h + 1) * HD] = (
                both[h * TOK:(h + 1) * TOK].astype(jnp.bfloat16))

    for bit in DIRECT:
        direct(bit).wait_send()
    relay().wait_send()
    for i, (condition, _) in enumerate(children):
        @pl.when(condition)
        def _(i=i):
            down(i, FIRST).wait_send()


def solution(mesh):
    def on_device(queries, keyval):
        return pl.pallas_call(
            kernel,
            out_shape=jax.ShapeDtypeStruct(queries.shape, jnp.bfloat16),
            in_specs=[pl.BlockSpec(memory_space=pl.ANY)] * 2,
            out_specs=pl.BlockSpec(memory_space=pltpu.VMEM),
            scratch_shapes=[
                pltpu.VMEM((TOK, HEADS * HD), jnp.bfloat16),
                pltpu.VMEM((SLOTS, 2, TOK, HD), jnp.bfloat16),
                pltpu.VMEM((PAIRS, HD, PAIR), jnp.bfloat16),
                pltpu.VMEM((PAIRS, 1, PAIR), jnp.float32),
                pltpu.VMEM((PAIRS, 1, PAIR), jnp.float32),
                pltpu.VMEM((PAIRS, HD, PAIR), jnp.float32),
                pltpu.SemaphoreType.DMA((2,)),
                pltpu.SemaphoreType.DMA((9,)),
                pltpu.SemaphoreType.DMA((SLOTS,)),
                pltpu.SemaphoreType.DMA((22,)),
            ],
            compiler_params=pltpu.CompilerParams(collective_id=0, has_side_effects=True),
        )(queries, keyval)

    return jax.shard_map(
        on_device,
        mesh=mesh,
        in_specs=(P("seq", None), P(None, "seq", None)),
        out_specs=P("seq", None),
        check_vma=False,
    )
```

time: 502 us -> 46.7 us (0.09)
  the two profiles are of different devices: /device:TPU:1 before, /device:TPU:53 now
where the time goes in v1:
time: 46.7 us; the launch traced here: 46.5 us
  Pallas kernels  44.7 us (96%)
  local copies, waits for them, and re-layouts  1.77 us (4%)
    pallas_call x1, Pallas kernels, on_device(): pl.pallas_call(kernel, out_shape=jax.ShapeDtypeStruct(queries.shape, jnp....  44.7 us
    unnamed x1, local copies, waits for them, and re-layouts  1.77 us

profile of v1, /device:TPU:53, one launch (start us, length us, event | category | flops | bytes accessed | tf_op | source)
XLA Modules:
  0.0 46.5 jit_solution(4811964449626409867)
XLA Ops:
  0.0 44.7 %shard_map.28 = bf16[192,1024]{1,0:T(8,128)(2,1)} custom-call(bf16[192,1024]{1,0:T(8,128)(2,1)} %q_hbm.1, bf16[2,192,128]{2,1,0:T(8,128)(2,1)} %kv_hbm.1), custom_call_target="tpu_custom_call" | custom-call | tf_op jit(solution)/shard_map/pallas_call | solution.py:208
  44.7 1.8 %copy.4 = bf16[192,1024]{1,0:T(8,128)(2,1)} copy(bf16[192,1024]{1,0:T(8,128)(2,1)} %shard_map.28) | data formatting | bytes 786432

commit v2 on v0

v2 whole, which is shorter than its diff:
```python
import math

import jax
import jax.numpy as jnp
from jax import lax
from jax.experimental import pallas as pl
from jax.experimental.pallas import tpu as pltpu
from jax.sharding import PartitionSpec as P

HEADS = 8
HD = 128
TOK = 192
ROWS = HEADS * TOK
PAIR = 2 * TOK
TILE = 512
SLOTS = 11
FIRST = 10
SCALE = math.log2(math.e) / math.sqrt(HD)
BITS = 9
URGENT = (5, 4, 3, 2, 8, 1, 7, 0)
FAR = 6
NEAR = (0, 1, 7, 2, 8, 3, 4)
Z_EDGES = ((0, 4), (0, 12), (0, 2), (0, 14), (0, 1), (0, 15),
           (4, 8), (4, 7), (4, 6), (4, 5), (12, 10), (12, 11), (14, 13), (2, 3), (8, 9))
HALVES = 2
RELAY_TURN = 4
MESH = pl.DeviceIdType.MESH


def index_of(y, z, x, c):
    return ((y * 16 + z) * 4 + x) * 2 + c


def kernel(q_hbm, kv_hbm, out_ref, q_ref, kv_ref, qt_ref, m_ref, l_ref, acc_ref,
           load_sem, send_sem, recv_sem, tree_send, first_recv, ready_sem, child_sem, half_send, half_recv, relay_send):
    me = lax.axis_index("seq")
    c = me % 2
    x = (me // 2) % 4
    z = (me // 8) % 16
    y = me // 128
    is_root = me == 0
    base = c == 0
    plane = base & (z == 0)
    row = plane & (y == 0)

    def partner(bit):
        stride = 1 << bit
        return me + stride * (1 - 2 * ((me // stride) % 2))

    def is_low(bit):
        low = (me // (1 << bit)) % 2 == 0
        if bit == FAR:
            return low
        return (low & (me != 0)) | (me == (1 << bit))

    low = [is_low(bit) for bit in range(BITS)]

    far = index_of(y, z % 4 + 4 * (3 - z // 4), x, c)
    straight = (z >= 8) & (z < 12)
    relays = z < 12

    def target_of(bit):
        return far if bit == FAR else partner(bit)

    def signal(sem, target):
        pl.semaphore_signal(sem, inc=1, device_id=(target,), device_id_type=MESH)

    q_copy = pltpu.make_async_copy(q_hbm, q_ref, load_sem.at[0])
    own_copy = pltpu.make_async_copy(kv_hbm, kv_ref.at[0], load_sem.at[1])
    own_copy.start()
    q_copy.start()

    edges = [(is_root, index_of(0, 0, dx, 0), None) for dx in (2, 1, 3)]
    edges += [(row, index_of(dy, 0, x, 0), None) for dy in (2, 1, 3)]
    edges += [(base & (z == up), index_of(y, down, x, 0), child_sem.at[down]) for up, down in Z_EDGES]
    edges += [(base, me + 1, None)]

    z_up = jnp.int32(0)
    for up, down in Z_EDGES:
        z_up = jnp.where(z == down, up, z_up)
    z_parent = index_of(y, z_up, x, 0)
    z_child = base & (z != 0)
    flat_child = plane & jnp.logical_not(is_root)
    flat_parent = jnp.where(y != 0, index_of(0, 0, x, 0), 0)

    barrier = pltpu.get_barrier_semaphore()
    expected = jnp.where(straight, 1, 0) + jnp.where(z_child, 1, 0) + jnp.where(is_root, 3, 0) + jnp.where(row, 3, 0)
    for bit in range(BITS):
        expected = expected + jnp.where(low[bit], 0, 1)

        @pl.when(low[bit])
        def _(bit=bit):
            signal(barrier, target_of(bit))

    @pl.when(z < 4)
    def _():
        signal(barrier, partner(FAR))

    @pl.when(flat_child)
    def _():
        signal(barrier, flat_parent)

    for condition, target, said in edges:
        if said is not None:
            @pl.when(condition)
            def _(target=target):
                signal(barrier, target)

    def direct(bit):
        return pltpu.make_async_remote_copy(
            src_ref=kv_ref.at[0], dst_ref=kv_ref.at[1 + bit], send_sem=send_sem.at[bit],
            recv_sem=recv_sem.at[1 + bit], device_id=(partner(bit),), device_id_type=MESH)

    def split(half):
        return pltpu.make_async_remote_copy(
            src_ref=kv_ref.at[0, half], dst_ref=kv_ref.at[6, half], send_sem=half_send.at[half],
            recv_sem=half_recv.at[half], device_id=(partner(5),), device_id_type=MESH)

    def relay(half):
        return pltpu.make_async_remote_copy(
            src_ref=kv_ref.at[6, half], dst_ref=kv_ref.at[7, half], send_sem=relay_send.at[half],
            recv_sem=recv_sem.at[7], device_id=(far,), device_id_type=MESH)

    def send(bit):
        if bit == 5:
            for half in range(2):
                split(half).start()
        else:
            direct(bit).start()

    def down(i, half, slot):
        return pltpu.make_async_remote_copy(
            src_ref=kv_ref.at[slot, half], dst_ref=kv_ref.at[FIRST, half],
            send_sem=tree_send.at[i, half], recv_sem=first_recv.at[half],
            device_id=(edges[i][1],), device_id_type=MESH)

    def pass_down(half, slot):
        for i, (condition, _, said) in enumerate(edges):
            @pl.when(condition)
            def _(i=i, said=said):
                if said is not None and half == 0:
                    pl.semaphore_wait(said, 1)
                down(i, half, slot).start()

    def take_first():
        for half in range(HALVES):
            view = kv_ref.at[FIRST, half]
            pltpu.make_async_copy(view, view, first_recv.at[half]).wait()
            pass_down(half, FIRST)

    def arrived(slot):
        pltpu.make_async_copy(kv_ref.at[slot], kv_ref.at[slot], recv_sem.at[slot]).wait()

    def send_up(bit):
        @pl.when(low[bit])
        def _():
            pl.semaphore_wait(ready_sem.at[bit], 1)
            send(bit)

    def attend(slot, start=False):
        vt = kv_ref[slot, 1].T
        keys = kv_ref[slot, 0]
        tiles = [slice(t * TILE, (t + 1) * TILE) for t in range(ROWS // TILE)]

        def scores(cols):
            return jnp.dot(keys, qt_ref[:, cols], preferred_element_type=jnp.float32)

        def finish(cols, weights, fade):
            part = jnp.dot(vt, weights, preferred_element_type=jnp.float32)
            acc_ref[:, cols] = part if start else acc_ref[:, cols] * fade + part

        ahead = scores(tiles[0])
        held = None
        for t, cols in enumerate(tiles):
            s = ahead
            if t + 1 < len(tiles):
                ahead = scores(tiles[t + 1])
            if held is not None:
                finish(*held)
            top = jnp.max(s, axis=0, keepdims=True)
            fade = None
            if start:
                new = top
            else:
                old = m_ref[:, cols]
                new = jnp.maximum(old, top)
                fade = jnp.exp2((old - new) * SCALE)
            p = jnp.exp2((s - new) * SCALE)
            total = jnp.sum(p, axis=0, keepdims=True)
            m_ref[:, cols] = new
            l_ref[:, cols] = total if start else l_ref[:, cols] * fade + total
            held = (cols, p.astype(jnp.bfloat16), fade)
        finish(*held)

    own_copy.wait()
    @pl.when(expected > 0)
    def _():
        pl.semaphore_wait(barrier, expected)

    @pl.when(straight)
    def _():
        direct(FAR).start()

    for bit in URGENT + (FAR,):
        @pl.when(jnp.logical_not(low[bit]))
        def _(bit=bit):
            signal(ready_sem.at[bit], target_of(bit))

    @pl.when(z_child)
    def _():
        signal(child_sem.at[z], z_parent)

    root_copy = pltpu.make_async_copy(kv_ref.at[0], kv_ref.at[FIRST], load_sem.at[1])

    @pl.when(is_root)
    def _():
        for i, (condition, _, said) in enumerate(edges):
            if said is None:
                for half in range(HALVES):
                    down(i, half, 0).start()
        root_copy.start()

    for bit in URGENT:
        @pl.when(jnp.logical_not(low[bit]))
        def _(bit=bit):
            send(bit)

    q_copy.wait()
    for pair in range(HEADS // 2):
        both = jnp.concatenate(
            [q_ref[:, (2 * pair + h) * HD:(2 * pair + h + 1) * HD] for h in range(2)], axis=0)
        qt_ref[:, pair * PAIR:(pair + 1) * PAIR] = both.T
    attend(0, True)

    @pl.when(is_root)
    def _():
        root_copy.wait()

    for bit in NEAR:
        send_up(bit)

    early = plane & jnp.logical_not(is_root)
    middle = base & ((z == 4) | (z == 12) | (z == 2) | (z == 14))
    for turn, bit in enumerate(NEAR):
        arrived(1 + bit)
        attend(1 + bit)
        if turn == 1:
            send_up(5)

            @pl.when(is_root)
            def _():
                for i, (condition, _, said) in enumerate(edges):
                    if said is not None:
                        @pl.when(condition)
                        def _(i=i, said=said):
                            pl.semaphore_wait(said, 1)
                            for half in range(HALVES):
                                down(i, half, 0).start()

            @pl.when(early & row)
            def _():
                take_first()
        if turn == 3:
            @pl.when(early & jnp.logical_not(row))
            def _():
                take_first()
        if turn == RELAY_TURN:
            for half in range(2):
                view = kv_ref.at[6, half]
                pltpu.make_async_copy(view, view, half_recv.at[half]).wait()
                if half == 0:
                    @pl.when(z < 8)
                    def _():
                        pl.semaphore_wait(ready_sem.at[FAR], 1)

                @pl.when(relays)
                def _(half=half):
                    relay(half).start()

            @pl.when(middle)
            def _():
                take_first()

    attend(6)

    late = z >= 13
    for turn in range(2):
        slot = jnp.where(late, 7 if turn == 0 else FIRST, FIRST if turn == 0 else 7)

        @pl.when(slot == 7)
        def _():
            arrived(7)

        @pl.when((slot == FIRST) & jnp.logical_not(plane | middle))
        def _():
            take_first()

        attend(slot)

    for pair in range(HEADS // 2):
        cols = slice(pair * PAIR, (pair + 1) * PAIR)
        both = (acc_ref[:, cols] / l_ref[:, cols]).astype(jnp.bfloat16).T
        for h in range(2):
            out_ref[:, (2 * pair + h) * HD:(2 * pair + h + 1) * HD] = both[h * TOK:(h + 1) * TOK]

    for bit in URGENT:
        if bit == 5:
            for half in range(2):
                split(half).wait_send()
        else:
            direct(bit).wait_send()

    @pl.when(straight)
    def _():
        direct(FAR).wait_send()

    @pl.when(relays)
    def _():
        for half in range(2):
            relay(half).wait_send()

    for i, (condition, _, _) in enumerate(edges):
        @pl.when(condition)
        def _(i=i):
            for half in range(HALVES):
                down(i, half, FIRST).wait_send()


def solution(mesh):
    def on_device(queries, keyval):
        return pl.pallas_call(
            kernel,
            out_shape=jax.ShapeDtypeStruct(queries.shape, jnp.bfloat16),
            in_specs=[pl.BlockSpec(memory_space=pl.ANY)] * 2,
            out_specs=pl.BlockSpec(memory_space=pltpu.VMEM),
            scratch_shapes=[
                pltpu.VMEM((TOK, HEADS * HD), jnp.bfloat16),
                pltpu.VMEM((SLOTS, 2, TOK, HD), jnp.bfloat16),
                pltpu.VMEM((HD, ROWS), jnp.bfloat16),
                pltpu.VMEM((1, ROWS), jnp.float32),
                pltpu.VMEM((1, ROWS), jnp.float32),
                pltpu.VMEM((HD, ROWS), jnp.float32),
                pltpu.SemaphoreType.DMA((2,)),
                pltpu.SemaphoreType.DMA((BITS,)),
                pltpu.SemaphoreType.DMA((SLOTS,)),
                pltpu.SemaphoreType.DMA((len(Z_EDGES) + 7, HALVES)),
                pltpu.SemaphoreType.DMA((HALVES,)),
                pltpu.SemaphoreType.REGULAR((BITS,)),
                pltpu.SemaphoreType.REGULAR((16,)),
                pltpu.SemaphoreType.DMA((2,)),
                pltpu.SemaphoreType.DMA((2,)),
                pltpu.SemaphoreType.DMA((2,)),
            ],
            compiler_params=pltpu.CompilerParams(collective_id=0, has_side_effects=True),
        )(queries, keyval)

    return jax.shard_map(
        on_device,
        mesh=mesh,
        in_specs=(P("seq", None), P(None, "seq", None)),
        out_specs=P("seq", None),
        check_vma=False,
    )
```

time: 502 us -> 33.4 us (0.07)
  the two profiles are of different devices: /device:TPU:1 before, /device:TPU:299 now
where the time goes in v2:
time: 33.4 us; the launch traced here: 33.3 us
  Pallas kernels  31.5 us (94%)
  local copies, waits for them, and re-layouts  1.77 us (5%)
    pallas_call x1, Pallas kernels, on_device(): pl.pallas_call(kernel, out_shape=jax.ShapeDtypeStruct(queries.shape, jnp....  31.5 us
    unnamed x1, local copies, waits for them, and re-layouts  1.77 us

profile of v2, /device:TPU:299, one launch (start us, length us, event | category | flops | bytes accessed | tf_op | source)
XLA Modules:
  0.0 33.3 jit_solution(4971382792754758611)
XLA Ops:
  0.0 31.5 %shard_map.28 = bf16[192,1024]{1,0:T(8,128)(2,1)} custom-call(bf16[192,1024]{1,0:T(8,128)(2,1)} %q_hbm.1, bf16[2,192,128]{2,1,0:T(8,128)(2,1)} %kv_hbm.1), custom_call_target="tpu_custom_call" | custom-call | tf_op jit(solution)/shard_map/pallas_call | solution.py:331
  31.5 1.8 %copy.4 = bf16[192,1024]{1,0:T(8,128)(2,1)} copy(bf16[192,1024]{1,0:T(8,128)(2,1)} %shard_map.28) | data formatting | bytes 786432

commit v3 on v2

--- a/solution.py
+++ b/solution.py
@@ -85,7 +85,7 @@
 
     barrier = pltpu.get_barrier_semaphore()
     expected = jnp.where(straight, 1, 0) + jnp.where(z_child, 1, 0) + jnp.where(is_root, 3, 0) + jnp.where(row, 3, 0)
-    for bit in range(BITS):
+    for bit in (5, FAR, 4, 3, 2, 8, 1, 7, 0):
         expected = expected + jnp.where(low[bit], 0, 1)
 
         @pl.when(low[bit])
@@ -241,12 +241,11 @@
 
     early = plane & jnp.logical_not(is_root)
     middle = base & ((z == 4) | (z == 12) | (z == 2) | (z == 14))
+    soon = base & (z == 8)
     for turn, bit in enumerate(NEAR):
         arrived(1 + bit)
         attend(1 + bit)
         if turn == 1:
-            send_up(5)
-
             @pl.when(is_root)
             def _():
                 for i, (condition, _, said) in enumerate(edges):
@@ -257,13 +256,19 @@
                             for half in range(HALVES):
                                 down(i, half, 0).start()
 
-            @pl.when(early & row)
+        if turn in (1, 3, RELAY_TURN):
+            now = early & row if turn == 1 else early & jnp.logical_not(row) if turn == 3 else middle
+
+            @pl.when(now)
             def _():
                 take_first()
-        if turn == 3:
-            @pl.when(early & jnp.logical_not(row))
+        if turn in (1, 3):
+            last = early & jnp.logical_not(row)
+
+            @pl.when(low[5] & (last if turn == 3 else jnp.logical_not(last)))
             def _():
-                take_first()
+                pl.semaphore_wait(ready_sem.at[5], 1)
+                send(5)
         if turn == RELAY_TURN:
             for half in range(2):
                 view = kv_ref.at[6, half]
@@ -277,7 +282,7 @@
                 def _(half=half):
                     relay(half).start()
 
-            @pl.when(middle)
+            @pl.when(soon)
             def _():
                 take_first()
 
@@ -291,7 +296,7 @@
         def _():
             arrived(7)
 
-        @pl.when((slot == FIRST) & jnp.logical_not(plane | middle))
+        @pl.when((slot == FIRST) & jnp.logical_not(plane | middle | soon))
         def _():
             take_first()
 
@@ -331,7 +336,7 @@
         return pl.pallas_call(
             kernel,
             out_shape=jax.ShapeDtypeStruct(queries.shape, jnp.bfloat16),
-            in_specs=[pl.BlockSpec(memory_space=pl.ANY)] * 2,
+            in_specs=[pl.BlockSpec(memory_space=pltpu.HBM)] * 2,
             out_specs=pl.BlockSpec(memory_space=pltpu.VMEM),
             scratch_shapes=[
                 pltpu.VMEM((TOK, HEADS * HD), jnp.bfloat16),
@@ -351,8 +356,9 @@
                 pltpu.SemaphoreType.DMA((2,)),
                 pltpu.SemaphoreType.DMA((2,)),
             ],
-            compiler_params=pltpu.CompilerParams(collective_id=0, has_side_effects=True),
-        )(queries, keyval)
+            compiler_params=pltpu.CompilerParams(
+                collective_id=0, has_side_effects=True, vmem_limit_bytes=16 << 20),
+        )(*(pltpu.with_memory_space_constraint(a, pltpu.HBM) for a in (queries, keyval)))
 
     return jax.shard_map(
         on_device,

time: 33.4 us -> 31.5 us (0.943)
  local copies, waits for them, and re-layouts: 1.77 us -> 0.75 us
  Pallas kernels: 31.5 us -> 30.7 us
    unnamed x1, local copies, waits for them, and re-layouts: 1.77 us -> 0.75 us
    pallas_call x1, Pallas kernels: 31.5 us -> 30.7 us  [on_device(): pl.pallas_call(kernel, out_shape=jax.ShapeDtypeStruct(queries.shape, jnp....]
where the time goes in v3:
time: 31.5 us; the launch traced here: 31.4 us
  Pallas kernels  30.7 us (97%)
  local copies, waits for them, and re-layouts  0.75 us (2%)
    pallas_call x1, Pallas kernels, on_device(): pl.pallas_call(kernel, out_shape=jax.ShapeDtypeStruct(queries.shape, jnp....  30.7 us
    unnamed x1, local copies, waits for them, and re-layouts  0.75 us

profile of v3, /device:TPU:299, one launch (start us, length us, event | category | flops | bytes accessed | tf_op | source)
XLA Modules:
  0.0 31.4 jit_solution(18349023801788825882)
XLA Ops:
  0.0 30.7 %shard_map.28 = bf16[192,1024]{1,0:T(8,128)(2,1)S(1)} custom-call(bf16[192,1024]{1,0:T(8,128)(2,1)} %q_hbm.1, bf16[2,192,128]{2,1,0:T(8,128)(2,1)} %kv_hbm.1), custom_call_target="tpu_custom_call" | custom-call | tf_op jit(solution)/shard_map/pallas_call | solution.py:336
  30.7 0.7 %copy.4 = bf16[192,1024]{1,0:T(8,128)(2,1)} copy(bf16[192,1024]{1,0:T(8,128)(2,1)S(1)} %shard_map.28) | data formatting | bytes 786432
